TPU v7x, 32 devices: a whole 2x2x4 slice. The times are simulated.
32 devices in a mesh: row: 8 (over z, x), col: 4 (over y, core).
Axes of the slice: x: 2, y: 2, z: 4, core: 2. Of those that a mesh axis runs over, the one named last changes fastest.
Arguments:
- geneo_vectors: bfloat16 [32, 32, 512, 512], P(None, None, 'row', 'col'), as said below
- phase_labels: int32 [32, 512, 512], P(None, 'row', 'col'), may hold values from 0 to 3, as said below
- phase_mobility: float32 [4], replicated, may hold values from 0.5 to 5
Outputs:
- coarse_factor: float32 [32, 4, 4, 2, 2, 8, 2, 32], P(None, None, 'col', None, None, 'row')
Inputs may be any that keep to these rules, and one draw needn't show every extreme that they name: `geneo_vectors`: the 32 vectors of each subdomain are linearly independent on its cells. `phase_labels`: within one subdomain the labels take one or two values, some q and (q + 1) modulo 4.
All inputs are finite; a program needn't handle non-finite values.
Results may differ from a plain program's by a relative error of at most 0.00055.
Values may be sent and summed in bfloat16 or wider, within the bound.
A program may use at most 512 MiB of HBM per device.

v0:
```python
import jax
import jax.numpy as jnp
from jax import lax
from jax.sharding import PartitionSpec as P

NB = 2
PSUB = 2


FACES = ((-1, 0), (1, 0), (0, -1), (0, 1))


def with_halo(cells, sides, width):
    for axis, dim in sides:
        count = lax.axis_size(axis)
        ends = count - 1
        head = lax.slice_in_dim(cells, 0, width, axis=dim)
        tail = lax.slice_in_dim(cells, cells.shape[dim] - width, cells.shape[dim], axis=dim)
        cells = jnp.concatenate(
            [
                lax.ppermute(tail, axis, [(i, (i + 1) % count) for i in range(ends)]),
                cells,
                lax.ppermute(head, axis, [((i + 1) % count, i) for i in range(ends)]),
            ],
            axis=dim,
        )
    return cells


def slot_offsets():
    offsets = [((0, 0), (0, 0))]
    for face in FACES:
        offsets += [((0, 0), face), (face, (0, 0)), (face, face)]
    for face_x in FACES[:2]:
        for face_y in FACES[2:]:
            offsets += [(face_x, face_y), (face_y, face_x)]
    return offsets


def band_index(from_off, to_off):
    return (to_off[0] - from_off[0] + 1) * 3 + (to_off[1] - from_off[1] + 1)


def from_next(field, axis):
    count = field.shape[axis]
    inner = lax.slice_in_dim(field, 1, count, axis=axis)
    blank = jnp.zeros_like(lax.slice_in_dim(field, 0, 1, axis=axis))
    return jnp.concatenate([inner, blank], axis=axis)


def from_prev(field, axis):
    count = field.shape[axis]
    inner = lax.slice_in_dim(field, 0, count - 1, axis=axis)
    blank = jnp.zeros_like(lax.slice_in_dim(field, 0, 1, axis=axis))
    return jnp.concatenate([blank, inner], axis=axis)


def laplace_own(own):
    field = own.astype(jnp.float32)
    near = from_next(field, 1) + from_prev(field, 1)
    near = near + from_next(field, 2) + from_prev(field, 2)
    near = near + from_next(field, 3) + from_prev(field, 3)
    return near - 6.0 * field


def contract_cells(left, right):
    flat_left = left.reshape(left.shape[0], -1)
    flat_right = right.reshape(right.shape[0], -1)
    return lax.dot_general(
        flat_left, flat_right, (((1,), (1,)), ((), ())), preferred_element_type=jnp.float32
    )


def local_tiles(own, labels, mobility_table):
    rims_x = jnp.stack([own[:, :, 0, :], own[:, :, -1, :]], axis=2)
    wide_x = with_halo(rims_x, (("row", 2),), 1)
    rims_y = jnp.stack([own[:, :, :, 0], own[:, :, :, -1]], axis=2)
    wide_y = with_halo(rims_y, (("col", 2),), 1)
    lower_x = wide_x[:, :, 0, :]
    upper_x = wide_x[:, :, 3, :]
    lower_y = wide_y[:, :, 0, :]
    upper_y = wide_y[:, :, 3, :]
    root_table = jnp.sqrt(mobility_table)
    cell_root = jnp.zeros(labels.shape, jnp.float32)
    for phase in range(mobility_table.shape[0]):
        cell_root = cell_root + jnp.where(labels == phase, root_table[phase], jnp.float32(0.0))
    flux = (laplace_own(own) * cell_root).astype(jnp.bfloat16)
    tiles = [contract_cells(own, own) + contract_cells(flux, flux)]
    face_data = [
        (flux[:, :, 0, :], lower_x, cell_root[:, 0, :]),
        (flux[:, :, -1, :], upper_x, cell_root[:, -1, :]),
        (flux[:, :, :, 0], lower_y, cell_root[:, :, 0]),
        (flux[:, :, :, -1], upper_y, cell_root[:, :, -1]),
    ]
    for layer_f, layer_z, layer_r in face_data:
        across = (layer_z.astype(jnp.float32) * layer_r).astype(jnp.bfloat16)
        cross = contract_cells(layer_f, across)
        tiles += [cross, cross.T, contract_cells(across, across)]
    for x_first in (True, False):
        for y_first in (True, False):
            layer_x = lower_x if x_first else upper_x
            layer_y = lower_y if y_first else upper_y
            cell_x = 0 if x_first else -1
            cell_y = 0 if y_first else -1
            corner_r = cell_root[:, cell_x, cell_y]
            along_x = (layer_x[:, :, cell_y].astype(jnp.float32) * corner_r).astype(jnp.bfloat16)
            along_y = (layer_y[:, :, cell_x].astype(jnp.float32) * corner_r).astype(jnp.bfloat16)
            pair = contract_cells(along_x, along_y)
            tiles += [pair, pair.T]
    return jnp.stack(tiles)


def shift_grid(values, offset):
    widths = [(1, 1), (1, 1)] + [(0, 0)] * (values.ndim - 2)
    padded = jnp.pad(values, widths)
    start_x = 1 - offset[0]
    start_y = 1 - offset[1]
    return padded[start_x : start_x + values.shape[0], start_y : start_y + values.shape[1]]


def to_owner(stack, n_row, n_col):
    slots = stack.shape[0]
    vectors = stack.shape[1]
    row_blocks = vectors // (NB * n_row)
    col_blocks = vectors // (NB * n_col)
    split = stack.reshape(slots, row_blocks, n_row, NB, col_blocks, n_col, NB)
    moved = split.transpose(2, 5, 0, 4, 6, 1, 3)
    return moved.reshape(n_row, n_col, slots * col_blocks * NB * row_blocks * NB)


def place_bands(bands, n_row, n_col):
    n_sub = n_row * n_col
    sub_x = jnp.arange(n_sub, dtype=jnp.int32) // n_col
    sub_y = jnp.arange(n_sub, dtype=jnp.int32) % n_col
    total = None
    for index in range(9):
        step_x = index // 3 - 1
        step_y = index % 3 - 1
        match = (
            (sub_x[:, None] == sub_x[None, :] + step_x)
            & (sub_y[:, None] == sub_y[None, :] + step_y)
        ).astype(jnp.float32)
        flat = bands[index].reshape(n_sub, -1).T
        term = match[:, None, :] * flat[None, :, :]
        total = term if total is None else total + term
    return total


def body(geneo_vectors, phase_labels, phase_mobility):
    vectors = geneo_vectors.shape[0]
    n_row = lax.axis_size("row")
    n_col = lax.axis_size("col")
    n_sub = n_row * n_col
    row_blocks = vectors // (NB * n_row)
    col_blocks = vectors // (NB * n_col)
    rows_here = row_blocks * NB * n_sub
    piece_len = col_blocks * NB * row_blocks * NB
    width = PSUB * vectors
    tiles = local_tiles(geneo_vectors, phase_labels, phase_mobility)
    offsets = slot_offsets()
    routed = lax.all_to_all(
        lax.all_to_all(
            to_owner(tiles, n_row, n_col), "row", split_axis=0, concat_axis=0, tiled=True
        ),
        "col",
        split_axis=1,
        concat_axis=1,
        tiled=True,
    )
    routed = routed.reshape(n_row, n_col, len(offsets), piece_len)
    bands = [jnp.zeros((n_row, n_col, piece_len), jnp.float32) for count in range(9)]
    for slot, pair_off in enumerate(offsets):
        place = band_index(pair_off[0], pair_off[1])
        bands[place] = bands[place] + shift_grid(routed[:, :, slot], pair_off[0])
    local = place_bands(bands, n_row, n_col).reshape(n_sub, col_blocks * NB, rows_here)
    col_index = lax.axis_index("col")
    row_sub = jnp.arange(rows_here, dtype=jnp.int32) % n_sub
    col_sub = jnp.arange(n_sub, dtype=jnp.int32)
    for panel in range(2):
        first = panel * PSUB
        last = first + PSUB
        part = local[first:last].reshape(PSUB, col_blocks, 1, NB, rows_here)
        whole = lax.all_gather(part, "col", axis=2, tiled=True).reshape(width, rows_here)
        diag_part = whole.reshape(width, row_blocks, 1, NB, n_sub)[:, :, :, :, first:last]
        diag_all = lax.all_gather(diag_part, "row", axis=2, tiled=True)
        diag = diag_all.transpose(0, 4, 1, 2, 3).reshape(width, width).T
        low = jnp.linalg.cholesky(diag)
        solved = lax.linalg.triangular_solve(low, whole, left_side=True, lower=True)
        solved = jnp.where(row_sub[None, :] >= first, solved, jnp.float32(0.0))
        mine = lax.dynamic_index_in_dim(
            solved.reshape(PSUB, col_blocks, n_col, NB, rows_here), col_index, 2, keepdims=False
        )
        local = local.at[first:last].set(mine.reshape(PSUB, col_blocks * NB, rows_here))
        gathered = lax.all_gather(
            solved.reshape(width, row_blocks, 1, NB, n_sub).astype(jnp.bfloat16),
            "row",
            axis=2,
            tiled=True,
        ).astype(jnp.float32)
        picked = lax.dynamic_index_in_dim(
            gathered.reshape(width, row_blocks, n_row // n_col, n_col, NB, n_sub),
            col_index,
            3,
            keepdims=False,
        )
        columns = (
            picked.reshape(width, col_blocks, NB, n_sub)
            .transpose(0, 3, 1, 2)
            .reshape(width, n_sub * col_blocks * NB)
        )
        update = lax.dot_general(
            columns,
            solved,
            (((0,), (0,)), ((), ())),
            precision=lax.Precision.HIGHEST,
            preferred_element_type=jnp.float32,
        )
        update = update.reshape(n_sub, col_blocks * NB, rows_here)
        trailing = (col_sub >= last)[:, None, None]
        above = (row_sub < last)[None, None, :]
        local = jnp.where(trailing, jnp.where(above, jnp.float32(0.0), local - update), local)
    return local.reshape(n_sub, col_blocks, 1, NB, row_blocks, 1, NB, n_sub)


def solution(mesh):
    return jax.shard_map(
        body,
        mesh=mesh,
        in_specs=(P(None, None, "row", "col"), P(None, "row", "col"), P()),
        out_specs=P(None, None, "col", None, None, "row", None, None),
        check_vma=False,
    )
```

profile of v0, /device:TPU:0, one launch (start us, length us, event | category | flops | bytes accessed | tf_op | source)
XLA Modules:
  0.0 737.6 jit_solution(1888599617356064845)
XLA Ops:
  0.0 25.4 %fusion.90 = (bf16[32,32,64,1]{3,2,1,0:T(8,128)(2,1)}, bf16[32,32,64,1]{3,2,1,0:T(8,128)(2,1)}) fusion(bf16[32,32,64,128]{3,2,1,0:T(8,128)(2,1)} %param.10), kind=kLoop, calls=%fused_computation.168 | loop fusion | bytes 524288 | tf_op jit(solution)/shard_map/slice | solution.py:77
  25.4 19.4 %copy.541 = bf16[32,32,64,1]{1,0,2,3:T(8,128)(2,1)} copy(bf16[32,32,64,1]{3,2,1,0:T(8,128)(2,1)} %get-tuple-element.42) | data formatting | bytes 262144
  48.0 19.4 %copy.542 = bf16[32,32,64,1]{1,0,2,3:T(8,128)(2,1)} copy(bf16[32,32,64,1]{3,2,1,0:T(8,128)(2,1)} %get-tuple-element.41) | data formatting | bytes 262144
  74.8 5.5 collective-permute-start
  80.3 21.9 %copy_convert_fusion = f32[32,32,64,128]{3,0,1,2:T(8,128)} fusion(bf16[32,32,64,128]{3,2,1,0:T(8,128)(2,1)} %param.10), kind=kLoop, calls=%fused_computation.3 | loop fusion | flops 8388608 | bytes 50331648 | tf_op jit(solution)/shard_map/convert_element_type | solution.py:59
  102.2 45.9 %fusion.89 = (f32[32,32,64,127]{3,0,1,2:T(8,128)}, f32[32,32,64,127]{3,0,1,2:T(8,128)}) fusion(f32[32,32,64,128]{3,0,1,2:T(8,128)} %copy_convert_fusion), kind=kLoop, calls=%fused_computation.167 | loop fusion | bytes 133169152 | tf_op jit(solution)/shard_map/slice | solution.py:46
  148.1 44.0 %fusion.88 = (f32[32,32,63,128]{3,0,1,2:T(8,128)}, f32[32,32,63,128]{3,0,1,2:T(8,128)}) fusion(f32[32,32,64,128]{3,0,1,2:T(8,128)} %copy_convert_fusion), kind=kLoop, calls=%fused_computation.166 | loop fusion | bytes 132120576 | tf_op jit(solution)/shard_map/slice | solution.py:46
  192.1 41.5 %fusion.87 = (f32[32,31,64,128]{3,0,1,2:T(8,128)}, f32[32,31,64,128]{3,0,1,2:T(8,128)}) fusion(f32[32,32,64,128]{3,0,1,2:T(8,128)} %copy_convert_fusion), kind=kLoop, calls=%fused_computation.165 | loop fusion | bytes 130023424 | tf_op jit(solution)/shard_map/slice | solution.py:46
  238.5 34.2 %fusion.8 = f32[32,32]{1,0:T(8,128)S(1)} fusion(bf16[32,32,64,128]{3,2,1,0:T(8,128)(2,1)} %param.10), kind=kOutput, calls=%fused_computation.18 | convolution fusion | flops 536870912 | bytes 16781312 | tf_op jit(solution)/shard_map/dot_general | solution.py:69
  273.4 71.5 %multiply_convert_fusion = bf16[32,32,64,128]{3,0,1,2:T(8,128)(2,1)} fusion(f32[32,32,64,127]{3,0,1,2:T(8,128)} %get-tuple-element.40, f32[32,32,64,127]{3,0,1,2:T(8,128)} %get-tuple-element.39, f32[32,32,63,128]{3,0,1,2:T(8,128)} %get-tuple-element.38, f32[32,32,63,128]{3,0,1,2:T(8,128)} %get-tuple-element.37, f32[32,31,64,128]{3,0,1,2:T(8,128)} %get-tuple-element.36, ...), kind=kLoop, calls=%fused_computation | loop fusion | flops 83886080 | bytes 232259584 | tf_op jit(solution)/shard_map/convert_element_type | solution.py:87
  344.9 25.9 %fusion.91 = (bf16[32,32,64,1]{3,0,1,2:T(8,128)(2,1)}, bf16[32,32,64,1]{3,0,1,2:T(8,128)(2,1)}) fusion(bf16[32,32,64,128]{3,0,1,2:T(8,128)(2,1)} %multiply_convert_fusion), kind=kLoop, calls=%fused_computation.169 | loop fusion | bytes 524288 | tf_op jit(solution)/shard_map/slice | solution.py:93
  370.8 13.5 %fusion.14 = f32[32,32]{1,0:T(8,128)} fusion(f32[32,32]{1,0:T(8,128)S(1)} %fusion.8, bf16[32,32,64,128]{3,0,1,2:T(8,128)(2,1)} %multiply_convert_fusion), kind=kOutput, calls=%fused_computation.20 | convolution fusion | flops 536871936 | bytes 16785408 | tf_op jit(solution)/shard_map/dot_general | solution.py:69
  385.6 21.2 %copy.385 = bf16[32,32,64,1]{2,1,0,3:T(8,128)(2,1)S(1)} copy(bf16[32,32,64,1]{3,0,1,2:T(8,128)(2,1)} %get-tuple-element.44) | data formatting | bytes 262144 | tf_op jit(solution)/shard_map/slice | solution.py:92
  407.5 21.4 %copy.393 = bf16[32,32,64,1]{2,1,0,3:T(8,128)(2,1)S(1)} copy(bf16[32,32,64,1]{3,0,1,2:T(8,128)(2,1)} %get-tuple-element.43) | data formatting | bytes 262144 | tf_op jit(solution)/shard_map/slice | solution.py:93
  534.9 7.7 %stack.75 = f32[21,2,8,2,4,4,2]{0,2,6,5,4,3,1:T(8,128)} concatenate(f32[1,2,8,2,4,4,2]{0,2,6,5,4,3,1:T(8,128)S(1)} %copy.408, f32[1,2,8,2,4,4,2]{0,2,6,5,4,3,1:T(8,128)} %copy.409, f32[1,2,8,2,4,4,2]{0,2,6,5,4,3,1:T(8,128)} %copy.410, f32[1,2,8,2,4,4,2]{0,2,6,5,4,3,1:T(8,128)} %copy.411, f32[1,2,8,2,4,4,2]{0,2,6,5,4,3,1:T(8,128)} %copy.412, f32[1,2,8,2,4,4,2]{0,2,6,5,4,3,1:T(8,128)} %copy.413, ...), dimensions={0} | concatenate | bytes 172032 | tf_op jit(solution)/shard_map/stack | solution.py:110
  546.5 5.5 all-to-all-start
  575.7 5.2 all_gather.18
  581.1 31.4 %all_gather.19 = f32[64,2,8,2,2]{0,4,3,1,2:T(2,128)S(1)} all-gather(f32[64,2,1,2,2]{0,4,3,1,2:T(2,128)S(1)} %copy.471), channel_id=1, replica_groups=mesh['row'=8,'col'=4] {'row'}, dimensions={2}, use_global_device_ids=true | all-gather | bytes 18432 | tf_op jit(solution)/shard_map/all_gather | solution.py:185
  612.6 5.8 cholesky.44
  625.0 30.7 %all_gather.20 = bf16[64,2,8,2,32]{0,4,3,1,2:T(8,128)(2,1)S(1)} all-gather(bf16[64,2,1,2,32]{0,4,3,1,2:T(8,128)(2,1)S(1)} %bitcast.334), channel_id=1, replica_groups=mesh['row'=8,'col'=4] {'row'}, dimensions={2}, use_global_device_ids=true | all-gather | bytes 147456 | tf_op jit(solution)/shard_map/all_gather | solution.py:194
  656.2 5.2 all_gather.21
  661.8 30.6 %all_gather.22 = f32[64,2,8,2,2]{0,4,3,1,2:T(2,128)S(1)} all-gather(f32[64,2,1,2,2]{0,4,3,1,2:T(2,128)S(1)} %copy.479), channel_id=1, replica_groups=mesh['row'=8,'col'=4] {'row'}, dimensions={2}, use_global_device_ids=true | all-gather | bytes 18432 | tf_op jit(solution)/shard_map/all_gather | solution.py:185
  692.6 5.8 cholesky.55
  705.0 30.7 %all_gather.23 = bf16[64,2,8,2,32]{0,4,3,1,2:T(8,128)(2,1)S(1)} all-gather(bf16[64,2,1,2,32]{0,4,3,1,2:T(8,128)(2,1)S(1)} %bitcast.335), channel_id=1, replica_groups=mesh['row'=8,'col'=4] {'row'}, dimensions={2}, use_global_device_ids=true | all-gather | bytes 147456 | tf_op jit(solution)/shard_map/all_gather | solution.py:194
  (217 shorter events, 167.1 us)
Async XLA Ops:
  44.8 389.9 %collective-permute-start.2 = (bf16[32,32,1,64]{1,0,3,2:T(8,128)(2,1)}, bf16[32,32,1,64]{1,0,3,2:T(8,128)(2,1)}, u32[]{:S(2)}, u32[]{:S(2)}) collective-permute-start(bf16[32,32,1,64]{1,0,3,2:T(8,128)(2,1)} %bitcast.32), channel_id=1, source_target_pairs={{0,1},{1,2},{2,3},{4,5},{5,6},{6,7},{8,9},{9,10},{10,11},{12,13},{... | collective-permute-start | bytes 393224 | tf_op jit(solution)/shard_map/ppermute | solution.py:21
  67.3 369.4 %collective-permute-start.3 = (bf16[32,32,1,64]{1,0,3,2:T(8,128)(2,1)}, bf16[32,32,1,64]{1,0,3,2:T(8,128)(2,1)}, u32[]{:S(2)}, u32[]{:S(2)}) collective-permute-start(bf16[32,32,1,64]{1,0,3,2:T(8,128)(2,1)} %bitcast.43), channel_id=1, source_target_pairs={{1,0},{2,1},{3,2},{5,4},{6,5},{7,6},{9,8},{10,9},{11,10},{13,12},{... | collective-permute-start | bytes 393224 | tf_op jit(solution)/shard_map/ppermute | solution.py:23
  72.7 389.1 %collective-permute-start.1 = (bf16[32,32,1,128]{3,1,0,2:T(8,128)(2,1)}, bf16[32,32,1,128]{3,1,0,2:T(8,128)(2,1)}, u32[]{:S(2)}, u32[]{:S(2)}) collective-permute-start(bf16[32,32,1,128]{3,1,0,2:T(8,128)(2,1)} %copy.540), channel_id=1, source_target_pairs={{4,0},{8,4},{12,8},{16,12},{20,16},{24,20},{28,24},{5,1},{9,5},{13... | collective-permute-start | bytes 786440 | tf_op jit(solution)/shard_map/ppermute | solution.py:23
  74.8 397.9 %collective-permute-start = (bf16[32,32,1,128]{3,1,2,0:T(8,128)(2,1)}, bf16[32,32,1,128]{3,1,2,0:T(8,128)(2,1)}, u32[]{:S(2)}, u32[]{:S(2)}) collective-permute-start(bf16[32,32,1,128]{3,1,2,0:T(8,128)(2,1)} %copy.539), channel_id=1, source_target_pairs={{0,4},{4,8},{8,12},{12,16},{16,20},{20,24},{24,28},{1,5},{5,9},{9,... | collective-permute-start | bytes 786440 | tf_op jit(solution)/shard_map/ppermute | solution.py:21
  192.1 41.5 %copy-start.4 = (f32[4]{0:T(128)S(1)}, f32[4]{0:T(128)}, u32[]{:S(2)}) copy-start(f32[4]{0:T(128)} %param.12) | copy-start | bytes 52
  192.1 42.2 %copy-start = (s32[32,64,128]{2,1,0:T(8,128)S(1)}, s32[32,64,128]{2,1,0:T(8,128)}, u32[]{:S(2)}) copy-start(s32[32,64,128]{2,1,0:T(8,128)} %param.11) | copy-start | bytes 3145732
  440.2 85.3 %copy-start.1 = (f32[32]{0:T(128)S(1)}, f32[32]{0:T(128)}, u32[]{:S(2)}) copy-start(f32[32]{0:T(128)} %get-tuple-element.31) | copy-start | bytes 388
  441.1 183.6 %copy-start.3 = (pred[128]{0:T(512)(128)(4,1)S(1)}, pred[128]{0:T(512)(128)(4,1)}, u32[]{:S(2)}) copy-start(pred[128]{0:T(512)(128)(4,1)} %broadcast_compare_fusion.3) | copy-start | bytes 388
  448.3 207.7 %copy-start.2 = (pred[32]{0:T(512)(128)(4,1)S(1)}, pred[32]{0:T(512)(128)(4,1)}, u32[]{:S(2)}) copy-start(pred[32]{0:T(512)(128)(4,1)} %iota_compare_fusion.2) | copy-start | bytes 100
  546.5 16.6 %all-to-all-start = ((f32[8,4,672]{2,1,0:T(4,128)}), f32[8,4,672]{2,1,0:T(4,128)S(1)}, u32[]{:S(2)}, u32[]{:S(2)}) async-start(f32[8,4,672]{2,1,0:T(4,128)} %copy.430), calls=%async_computation | async-start | bytes 196608 | tf_op jit(solution)/shard_map/all_to_all | solution.py:162
  563.8 8.8 %all-to-all-start.1 = ((f32[8,4,672]{2,0,1:T(8,128)}), f32[8,4,672]{2,0,1:T(8,128)S(1)}, u32[]{:S(2)}, u32[]{:S(2)}) async-start(f32[8,4,672]{2,0,1:T(8,128)} %copy.431), calls=%async_computation.1 | async-start | bytes 196608 | tf_op jit(solution)/shard_map/all_to_all | solution.py:161
where the time goes:
time: 749 us; the launch traced here: 738 us
  local copies, waits for them, and re-layouts  388 us (52%)
  blocking collectives  134 us (18%)
  other arithmetic  130 us (17%)
  matrix products  59.1 us (8%)
  starting transfers between devices  21.3 us (3%)
    slice x3, local copies, waits for them, and re-layouts, from_next(): inner = lax.slice_in_dim(field, 1, count, axis=axis)  131 us
    another operation x35, local copies, waits for them, and re-layouts, local_tiles(): return jnp.stack(tiles)  77.4 us
    convert_element_type x1, other arithmetic, local_tiles(): flux = (laplace_own(own) * cell_root).astype(jnp.bfloat16)  71.5 us
    all_gather x2, blocking collectives, body(): diag_all = lax.all_gather(diag_part, 'row', axis=2, tiled=True)  62 us
    all_gather x2, blocking collectives, body(): lax.all_gather(solved.reshape(width, row_blocks, 1, NB, n_sub).astype(jnp...  61.5 us
    dot_general x14, matrix products, contract_cells(): lax.dot_general(flat_left, flat_right, (((1,), (1,)), ((), ())), preferre...  58.3 us
    slice x2, local copies, waits for them, and re-layouts, local_tiles(): flux[:, :, :, -1]  47.3 us
    unnamed x16, local copies, waits for them, and re-layouts  41.7 us
  transfers between devices with their start and end apart: 6, of which 1 were waited for; matrix products, arithmetic and copies ran while one was open for 58% of the time, Pallas kernels for 0%

commit v1 on v0

--- a/solution.py
+++ b/solution.py
@@ -1,6 +1,8 @@
 import jax
 import jax.numpy as jnp
 from jax import lax
+from jax.experimental import pallas as pl
+from jax.experimental.pallas import tpu as pltpu
 from jax.sharding import PartitionSpec as P
 
 NB = 2
@@ -71,26 +73,113 @@
     )
 
 
+SUBL = 16
+
+
+def flux_gram_kernel(prev_ref, cur_ref, next_ref, root_ref, acc_ref, fx_ref, edge_ref, flux_ref):
+    z = pl.program_id(0)
+    n_z = pl.num_programs(0)
+    vectors, n_x, n_y = flux_ref.shape
+    half = n_y // 2
+
+    @pl.when(z == 0)
+    def _():
+        acc_ref[...] = jnp.zeros_like(acc_ref)
+        edge_ref[...] = jnp.zeros_like(edge_ref)
+
+    use_prev = (z > 0).astype(jnp.float32)
+    use_next = (z < n_z - 1).astype(jnp.float32)
+
+    def step(v, carry):
+        rows = lax.broadcasted_iota(jnp.int32, (n_x, n_y), 0)
+        lanes = lax.broadcasted_iota(jnp.int32, (n_x, n_y), 1)
+        own = cur_ref[v, 0].astype(jnp.float32)
+        near = next_ref[v, 0].astype(jnp.float32) * use_next
+        near = near + prev_ref[v, 0].astype(jnp.float32) * use_prev
+        near = near + jnp.where(rows == n_x - 1, 0.0, pltpu.roll(own, n_x - 1, 0))
+        near = near + jnp.where(rows == 0, 0.0, pltpu.roll(own, 1, 0))
+        near = near + jnp.where(lanes == n_y - 1, 0.0, pltpu.roll(own, n_y - 1, 1))
+        near = near + jnp.where(lanes == 0, 0.0, pltpu.roll(own, 1, 1))
+        flux = ((near - 6.0 * own) * root_ref[0]).astype(jnp.bfloat16)
+        flux_ref[v] = flux
+        wide = flux.astype(jnp.float32)
+        fx_ref[v, 0, 0:1, :] = wide[0:1, :]
+        fx_ref[v, 0, 1:2, :] = wide[n_x - 1 : n_x, :]
+        turned_f = pltpu.roll(wide, 2 * z + 1, 1)
+        turned_o = pltpu.roll(own, 2 * z + 1 + half, 1)
+        kept = edge_ref[v]
+        is_f = (lanes >= 2 * z) & (lanes < 2 * z + 2)
+        is_o = (lanes >= 2 * z + half) & (lanes < 2 * z + 2 + half)
+        edge_ref[v] = jnp.where(is_f, turned_f, jnp.where(is_o, turned_o, kept))
+        return carry
+
+    lax.fori_loop(0, vectors, step, 0)
+    for block in range(n_x // SUBL):
+        span = slice(block * SUBL, (block + 1) * SUBL)
+        left = cur_ref[:, 0, span, :].reshape(vectors * SUBL, n_y)
+        right = flux_ref[:, span, :].reshape(vectors * SUBL, n_y)
+        both = jnp.concatenate([left, right], axis=1)
+        acc_ref[...] += lax.dot_general(
+            both, both, (((1,), (1,)), ((), ())), preferred_element_type=jnp.float32
+        )
+
+
+def flux_gram(own, cell_root):
+    vectors, n_z, n_x, n_y = own.shape
+    order = vectors * SUBL
+    block = (vectors, 1, n_x, n_y)
+    acc, flux_x, edges = pl.pallas_call(
+        flux_gram_kernel,
+        grid=(n_z,),
+        in_specs=[
+            pl.BlockSpec(block, lambda z: (0, jnp.maximum(z - 1, 0), 0, 0)),
+            pl.BlockSpec(block, lambda z: (0, z, 0, 0)),
+            pl.BlockSpec(block, lambda z: (0, jnp.minimum(z + 1, n_z - 1), 0, 0)),
+            pl.BlockSpec((1, n_x, n_y), lambda z: (z, 0, 0)),
+        ],
+        out_specs=[
+            pl.BlockSpec((order, order), lambda z: (0, 0)),
+            pl.BlockSpec((vectors, 1, 2, n_y), lambda z: (0, z, 0, 0)),
+            pl.BlockSpec((vectors, n_x, n_y), lambda z: (0, 0, 0)),
+        ],
+        out_shape=[
+            jax.ShapeDtypeStruct((order, order), jnp.float32),
+            jax.ShapeDtypeStruct((vectors, n_z, 2, n_y), jnp.float32),
+            jax.ShapeDtypeStruct((vectors, n_x, n_y), jnp.float32),
+        ],
+        scratch_shapes=[pltpu.VMEM((vectors, n_x, n_y), jnp.bfloat16)],
+        compiler_params=pltpu.CompilerParams(vmem_limit_bytes=40 * 1024 * 1024),
+    )(own, own, own, cell_root)
+    place = jnp.arange(order, dtype=jnp.int32) % SUBL
+    acc = jnp.where(place[:, None] == place[None, :], acc, jnp.float32(0.0))
+    half_sum = acc.reshape(vectors, SUBL, order).sum(1)
+    gram = half_sum.reshape(vectors, vectors, SUBL).sum(2)
+    half = n_y // 2
+    edges = edges.astype(jnp.bfloat16)
+    flux_edge = edges[:, :, : 2 * n_z].reshape(vectors, n_x, n_z, 2)
+    own_edge = edges[:, :, half : half + 2 * n_z].reshape(vectors, n_x, n_z, 2)
+    return gram, flux_x.astype(jnp.bfloat16), flux_edge, own_edge
+
+
 def local_tiles(own, labels, mobility_table):
     rims_x = jnp.stack([own[:, :, 0, :], own[:, :, -1, :]], axis=2)
     wide_x = with_halo(rims_x, (("row", 2),), 1)
-    rims_y = jnp.stack([own[:, :, :, 0], own[:, :, :, -1]], axis=2)
-    wide_y = with_halo(rims_y, (("col", 2),), 1)
     lower_x = wide_x[:, :, 0, :]
     upper_x = wide_x[:, :, 3, :]
-    lower_y = wide_y[:, :, 0, :]
-    upper_y = wide_y[:, :, 3, :]
     root_table = jnp.sqrt(mobility_table)
     cell_root = jnp.zeros(labels.shape, jnp.float32)
     for phase in range(mobility_table.shape[0]):
         cell_root = cell_root + jnp.where(labels == phase, root_table[phase], jnp.float32(0.0))
-    flux = (laplace_own(own) * cell_root).astype(jnp.bfloat16)
-    tiles = [contract_cells(own, own) + contract_cells(flux, flux)]
+    gram, flux_x, flux_edge, own_edge = flux_gram(own, cell_root)
+    tiles = [gram]
+    count = lax.axis_size("col")
+    lower_y = lax.ppermute(own_edge[..., 0], "col", [(i, i + 1) for i in range(count - 1)])
+    upper_y = lax.ppermute(own_edge[..., 1], "col", [(i + 1, i) for i in range(count - 1)])
     face_data = [
-        (flux[:, :, 0, :], lower_x, cell_root[:, 0, :]),
-        (flux[:, :, -1, :], upper_x, cell_root[:, -1, :]),
-        (flux[:, :, :, 0], lower_y, cell_root[:, :, 0]),
-        (flux[:, :, :, -1], upper_y, cell_root[:, :, -1]),
+        (flux_x[:, :, 0, :], lower_x, cell_root[:, 0, :]),
+        (flux_x[:, :, 1, :], upper_x, cell_root[:, -1, :]),
+        (flux_edge[..., 1], lower_y, cell_root[:, :, 0].T),
+        (flux_edge[..., 0], upper_y, cell_root[:, :, -1].T),
     ]
     for layer_f, layer_z, layer_r in face_data:
         across = (layer_z.astype(jnp.float32) * layer_r).astype(jnp.bfloat16)
@@ -104,7 +193,7 @@
             cell_y = 0 if y_first else -1
             corner_r = cell_root[:, cell_x, cell_y]
             along_x = (layer_x[:, :, cell_y].astype(jnp.float32) * corner_r).astype(jnp.bfloat16)
-            along_y = (layer_y[:, :, cell_x].astype(jnp.float32) * corner_r).astype(jnp.bfloat16)
+            along_y = (layer_y[:, cell_x, :].astype(jnp.float32) * corner_r).astype(jnp.bfloat16)
             pair = contract_cells(along_x, along_y)
             tiles += [pair, pair.T]
     return jnp.stack(tiles)
@@ -173,52 +262,65 @@
         place = band_index(pair_off[0], pair_off[1])
         bands[place] = bands[place] + shift_grid(routed[:, :, slot], pair_off[0])
     local = place_bands(bands, n_row, n_col).reshape(n_sub, col_blocks * NB, rows_here)
+    row_index = lax.axis_index("row")
     col_index = lax.axis_index("col")
     row_sub = jnp.arange(rows_here, dtype=jnp.int32) % n_sub
-    col_sub = jnp.arange(n_sub, dtype=jnp.int32)
+    ends = 2 * PSUB
+    mine = local[:ends].reshape(ends, col_blocks, NB, rows_here)
+    parts = lax.all_gather(mine, ("row", "col"), axis=0, tiled=False)
+    parts = parts.reshape(n_row, n_col, ends, col_blocks, NB, rows_here)
+    panels = parts.transpose(2, 3, 1, 4, 0, 5).reshape(2, width, n_row, rows_here)
+
+    def rows_of(block, first, last):
+        grid = block.reshape(width, n_row, row_blocks, NB, n_sub)[..., first:last]
+        return grid.transpose(0, 4, 2, 1, 3).reshape(width, (last - first) * vectors)
+
+    done = []
     for panel in range(2):
         first = panel * PSUB
         last = first + PSUB
-        part = local[first:last].reshape(PSUB, col_blocks, 1, NB, rows_here)
-        whole = lax.all_gather(part, "col", axis=2, tiled=True).reshape(width, rows_here)
-        diag_part = whole.reshape(width, row_blocks, 1, NB, n_sub)[:, :, :, :, first:last]
-        diag_all = lax.all_gather(diag_part, "row", axis=2, tiled=True)
-        diag = diag_all.transpose(0, 4, 1, 2, 3).reshape(width, width).T
-        low = jnp.linalg.cholesky(diag)
-        solved = lax.linalg.triangular_solve(low, whole, left_side=True, lower=True)
-        solved = jnp.where(row_sub[None, :] >= first, solved, jnp.float32(0.0))
-        mine = lax.dynamic_index_in_dim(
-            solved.reshape(PSUB, col_blocks, n_col, NB, rows_here), col_index, 2, keepdims=False
-        )
-        local = local.at[first:last].set(mine.reshape(PSUB, col_blocks * NB, rows_here))
-        gathered = lax.all_gather(
-            solved.reshape(width, row_blocks, 1, NB, n_sub).astype(jnp.bfloat16),
-            "row",
-            axis=2,
-            tiled=True,
-        ).astype(jnp.float32)
-        picked = lax.dynamic_index_in_dim(
-            gathered.reshape(width, row_blocks, n_row // n_col, n_col, NB, n_sub),
-            col_index,
-            3,
-            keepdims=False,
-        )
-        columns = (
-            picked.reshape(width, col_blocks, NB, n_sub)
-            .transpose(0, 3, 1, 2)
-            .reshape(width, n_sub * col_blocks * NB)
-        )
-        update = lax.dot_general(
-            columns,
-            solved,
-            (((0,), (0,)), ((), ())),
-            precision=lax.Precision.HIGHEST,
-            preferred_element_type=jnp.float32,
-        )
-        update = update.reshape(n_sub, col_blocks * NB, rows_here)
-        trailing = (col_sub >= last)[:, None, None]
-        above = (row_sub < last)[None, None, :]
-        local = jnp.where(trailing, jnp.where(above, jnp.float32(0.0), local - update), local)
+        block = panels[panel]
+        for solved in done:
+            change = lax.dot_general(
+                rows_of(solved, first, last),
+                solved.reshape(width, n_row * rows_here),
+                (((0,), (0,)), ((), ())),
+                precision=lax.Precision.HIGHEST,
+                preferred_element_type=jnp.float32,
+            )
+            block = block - change.reshape(width, n_row, rows_here)
+        block = jnp.where(row_sub >= first, block, jnp.float32(0.0))
+        low = jnp.linalg.cholesky(rows_of(block, first, last).T)
+        solved = lax.linalg.triangular_solve(
+            low, block.reshape(width, n_row * rows_here), left_side=True, lower=True
+        ).reshape(width, n_row, rows_here)
+        done.append(solved)
+    both = jnp.concatenate(done, axis=0)
+    rows_mine = lax.dynamic_index_in_dim(both, row_index, 1, keepdims=False)
+    by_block = both.reshape(2 * width, n_row, row_blocks, NB, n_sub).transpose(0, 2, 1, 3, 4)
+    picked = lax.dynamic_index_in_dim(
+        by_block.reshape(2 * width, row_blocks, n_row // n_col, n_col, NB, n_sub),
+        col_index,
+        3,
+        keepdims=False,
+    )
+    columns = (
+        picked.reshape(2 * width, col_blocks * NB, n_sub)
+        .transpose(0, 2, 1)
+        .reshape(2 * width, n_sub * col_blocks * NB)
+    )
+    update = lax.dot_general(
+        columns,
+        rows_mine,
+        (((0,), (0,)), ((), ())),
+        precision=lax.Precision.HIGHEST,
+        preferred_element_type=jnp.float32,
+    ).reshape(n_sub, col_blocks * NB, rows_here)
+    panel_mine = lax.dynamic_index_in_dim(
+        rows_mine.reshape(ends, col_blocks, n_col, NB, rows_here), col_index, 2, keepdims=False
+    ).reshape(ends, col_blocks * NB, rows_here)
+    rest = jnp.where(row_sub < ends, jnp.float32(0.0), local[ends:] - update[ends:])
+    local = jnp.concatenate([panel_mine, rest], axis=0)
     return local.reshape(n_sub, col_blocks, 1, NB, row_blocks, 1, NB, n_sub)
 
 

time: 749 us -> 460 us (0.61)
  local copies, waits for them, and re-layouts: 388 us -> 139 us
  Pallas kernels: 0 us -> 185 us
  blocking collectives: 134 us -> 38.5 us
  other arithmetic: 130 us -> 44.9 us
  matrix products: 59.1 us -> 12.4 us
    slice x17 -> x14, local copies, waits for them, and re-layouts: 231 us -> 11 us  [the longest x2 3.7 us: flux_gram(): own_edge = edges[:, :, half:half + 2 * n_z].reshape(vectors, n_x, n_z, 2)]
    pallas_call x0 -> x1, Pallas kernels: none -> 185 us  [flux_gram(): pl.pallas_call(flux_gram_kernel, grid=(n_z,), in_specs=[pl.BlockSpec(bloc...]
    all_gather x6 -> x1, blocking collectives: 134 us -> 38.5 us  [body(): parts = lax.all_gather(mine, ('row', 'col'), axis=0, tiled=False)]
    convert_element_type x2 -> x3, other arithmetic: 93.4 us -> 3.23 us  [the longest x1 2.7 us: local_tiles(): (layer_x[:, :, cell_y].astype(jnp.float32) * corner_r).astype(jnp.bfloat16)]
    dot_general x14 -> x12, matrix products: 58.3 us -> 10.9 us  [contract_cells(): lax.dot_general(flat_left, flat_right, (((1,), (1,)), ((), ())), preferre...]
    unnamed x16 -> x27, local copies, waits for them, and re-layouts: 41.7 us -> 6.83 us
    another operation x35 -> x39, local copies, waits for them, and re-layouts: 77.4 us -> 97.4 us  [local_tiles(): return jnp.stack(tiles)]
    mul x29 -> x0, local copies, waits for them, and re-layouts: 9.05 us -> none  [the longest x27 8.16 us: place_bands(): term = match[:, None, :] * flat[None, :, :]]
  transfers between devices with their start and end apart: 6 -> 6, of which waited for: 1 -> 2; matrix products, arithmetic and copies ran while one was open for 58% -> 19% of each run, Pallas kernels for 0% -> 41%
where the time goes in v1:
time: 460 us; the launch traced here: 455 us
  Pallas kernels  185 us (40%)
  local copies, waits for them, and re-layouts  139 us (30%)
  other arithmetic  44.9 us (10%)
  blocking collectives  38.5 us (8%)
  starting transfers between devices  22.6 us (5%)
  matrix products  12.4 us (3%)
  waiting for transfers between devices  10.8 us (2%)
    pallas_call x1, Pallas kernels, flux_gram(): pl.pallas_call(flux_gram_kernel, grid=(n_z,), in_specs=[pl.BlockSpec(bloc...  185 us
    another operation x39, local copies, waits for them, and re-layouts, local_tiles(): return jnp.stack(tiles)  97.4 us
    all_gather x1, blocking collectives, body(): parts = lax.all_gather(mine, ('row', 'col'), axis=0, tiled=False)  38.5 us
    another operation x6, other arithmetic, body(): low = jnp.linalg.cholesky(rows_of(block, first, last).T)  13 us
    another operation x4, other arithmetic, body(): lax.linalg.triangular_solve(low, block.reshape(width, n_row * rows_here),...  11.1 us
    dot_general x12, matrix products, contract_cells(): lax.dot_general(flat_left, flat_right, (((1,), (1,)), ((), ())), preferre...  10.9 us
  transfers between devices with their start and end apart: 6, of which 2 were waited for; matrix products, arithmetic and copies ran while one was open for 19% of the time, Pallas kernels for 41%

profile of v1, /device:TPU:0, one launch (start us, length us, event | category | flops | bytes accessed | tf_op | source)
XLA Modules:
  0.0 454.9 jit_solution(1287684262653949693)
XLA Ops:
  4.1 4.9 %collective-permute-start = (bf16[32,32,1,128]{3,1,0,2:T(8,128)(2,1)}, bf16[32,32,1,128]{3,1,0,2:T(8,128)(2,1)S(1)}, u32[]{:S(2)}, u32[]{:S(2)}) collective-permute-start(bf16[32,32,1,128]{3,1,0,2:T(8,128)(2,1)} %copy.489), channel_id=1, source_target_pairs={{0,4},{4,8},{8,12},{12,16},{16,20},{20,24},{24,28},{1,5},{5,9},{9,... | collective-permute-start | bytes 786440 | tf_op jit(solution)/shard_map/ppermute | solution.py:23
  12.4 4.2 select_add_fusion.root_ref
  16.5 185.3 %shard_map.37 = (f32[512,512]{1,0:T(8,128)S(1)}, f32[32,32,2,128]{3,2,1,0:T(2,128)S(1)}, f32[32,64,128]{2,1,0:T(8,128)S(1)}) custom-call(bf16[32,32,64,128]{3,2,1,0:T(8,128)(2,1)} %next_ref.1, bf16[32,32,64,128]{3,2,1,0:T(8,128)(2,1)} %next_ref.1, bf16[32,32,64,128]{3,2,1,0:T(8,128)(2,1)} %next_ref.1, f32[32,64,128]{2,1,0:T(8,128)S(1)} %select_add_fusion.root_ref), custom_call_target="tpu_custom_call" | custom-call | tf_op jit(solution)/shard_map/pallas_call | solution.py:131
  251.9 4.0 copy.381
  256.8 5.1 %copy.382 = f32[1,2,8,2,4,4,2]{0,2,6,5,4,3,1:T(8,128)} copy(f32[1,2,8,2,4,4,2]{3,2,1,6,5,4,0:T(8,128)} %stack.71) | data formatting | bytes 8192 | tf_op jit(solution)/shard_map/stack | solution.py:199
  263.1 5.1 %copy.383 = f32[1,2,8,2,4,4,2]{0,2,6,5,4,3,1:T(8,128)} copy(f32[1,2,8,2,4,4,2]{3,2,1,6,5,4,0:T(8,128)} %stack.72) | data formatting | bytes 8192 | tf_op jit(solution)/shard_map/stack | solution.py:199
  273.1 4.8 %copy.372 = f32[1,2,8,2,4,4,2]{0,2,6,5,4,3,1:T(8,128)} copy(f32[1,2,8,2,4,4,2]{6,5,4,3,2,1,0:T(4,128)} %reshape.893) | data formatting | bytes 8192 | tf_op jit(solution)/shard_map/stack | solution.py:199
  278.8 5.1 %copy.373 = f32[1,2,8,2,4,4,2]{0,2,6,5,4,3,1:T(8,128)} copy(f32[1,2,8,2,4,4,2]{3,2,1,6,5,4,0:T(8,128)} %stack.64) | data formatting | bytes 8192 | tf_op jit(solution)/shard_map/stack | solution.py:199
  291.1 4.8 %copy.375 = f32[1,2,8,2,4,4,2]{0,2,6,5,4,3,1:T(8,128)} copy(f32[1,2,8,2,4,4,2]{6,5,4,3,2,1,0:T(4,128)} %reshape.894) | data formatting | bytes 8192 | tf_op jit(solution)/shard_map/stack | solution.py:199
  296.8 5.1 %copy.376 = f32[1,2,8,2,4,4,2]{0,2,6,5,4,3,1:T(8,128)} copy(f32[1,2,8,2,4,4,2]{3,2,1,6,5,4,0:T(8,128)} %stack.66) | data formatting | bytes 8192 | tf_op jit(solution)/shard_map/stack | solution.py:199
  313.4 4.2 copy.385
  322.8 4.2 copy.387
  332.2 4.2 copy.389
  341.7 4.1 copy.391
  345.8 8.0 %stack.81 = f32[21,2,8,2,4,4,2]{0,2,6,5,4,3,1:T(8,128)} concatenate(f32[1,2,8,2,4,4,2]{0,2,6,5,4,3,1:T(8,128)S(1)} %copy.371, f32[1,2,8,2,4,4,2]{0,2,6,5,4,3,1:T(8,128)} %copy.372, f32[1,2,8,2,4,4,2]{0,2,6,5,4,3,1:T(8,128)} %copy.373, f32[1,2,8,2,4,4,2]{0,2,6,5,4,3,1:T(8,128)} %copy.374, f32[1,2,8,2,4,4,2]{0,2,6,5,4,3,1:T(8,128)} %copy.375, f32[1,2,8,2,4,4,2]{0,2,6,5,4,3,1:T(8,128)} %copy.376, ...), dimensions={0} | concatenate | bytes 172032 | tf_op jit(solution)/shard_map/stack | solution.py:199
  357.8 7.5 %all-to-all-start = ((f32[8,4,672]{2,1,0:T(4,128)}), f32[8,4,672]{2,1,0:T(4,128)S(1)}, u32[]{:S(2)}, u32[]{:S(2)}) async-start(f32[8,4,672]{2,1,0:T(4,128)} %copy.393), calls=%async_computation | async-start | bytes 196608 | tf_op jit(solution)/shard_map/all_to_all | solution.py:251
  365.9 6.5 %all-to-all-done = f32[8,4,672]{2,1,0:T(4,128)S(1)} async-done(((f32[8,4,672]{2,1,0:T(4,128)}), f32[8,4,672]{2,1,0:T(4,128)S(1)}, u32[]{:S(2)}, u32[]{:S(2)}) %all-to-all-start) | async-done | bytes 86048 | tf_op jit(solution)/shard_map/all_to_all | solution.py:251
  373.0 5.0 %all-to-all-start.1 = ((f32[8,4,672]{2,0,1:T(8,128)}), f32[8,4,672]{2,0,1:T(8,128)S(1)}, u32[]{:S(2)}, u32[]{:S(2)}) async-start(f32[8,4,672]{2,0,1:T(8,128)} %copy.394), calls=%async_computation.1 | async-start | bytes 196608 | tf_op jit(solution)/shard_map/all_to_all | solution.py:250
  378.0 4.3 all-to-all-done.1
  384.2 38.5 %all_gather.3 = f32[32,4,4,2,128]{4,2,3,1,0:T(4,128)S(1)} all-gather(f32[1,4,4,2,128]{4,2,3,1,0:T(4,128)S(1)} %copy.425), channel_id=1, replica_groups=mesh['row'=8,'col'=4] {'row','col'}, dimensions={0}, use_global_device_ids=true | all-gather | bytes 540672 | tf_op jit(solution)/shard_map/all_gather | solution.py:270
  425.4 5.8 %cholesky.44 = f32[64,64]{1,0:T(8,128)S(1)} custom-call(f32[64,64]{1,0:T(8,128)S(1)} %add_multiply_fusion.1), custom_call_target="Cholesky" | custom-call | tf_op jit(solution)/shard_map/jit(cholesky)/cholesky | solution.py:293
  432.6 4.9 %custom-call.6 = f32[1,64,64]{1,2,0:T(8,128)S(1)} custom-call(f32[1,64,64]{2,1,0:T(8,128)S(1)} %fusion.32), custom_call_target="InvertDiagBlocksLowerTriangular" | custom-call | tf_op jit(solution)/shard_map/triangular_solve/custom-call.0 | solution.py:294
  439.2 5.8 %cholesky.55 = f32[64,64]{1,0:T(8,128)S(1)} custom-call(f32[64,64]{1,0:T(8,128)S(1)} %add_multiply_fusion), custom_call_target="Cholesky" | custom-call | tf_op jit(solution)/shard_map/jit(cholesky)/cholesky | solution.py:293
  446.4 4.9 %custom-call.7 = f32[1,64,64]{1,2,0:T(8,128)S(1)} custom-call(f32[1,64,64]{2,1,0:T(8,128)S(1)} %fusion.33), custom_call_target="InvertDiagBlocksLowerTriangular" | custom-call | tf_op jit(solution)/shard_map/triangular_solve/custom-call.0 | solution.py:294
  (195 shorter events, 117.3 us)
Async XLA Ops:
  4.1 264.1 %collective-permute-start = (bf16[32,32,1,128]{3,1,0,2:T(8,128)(2,1)}, bf16[32,32,1,128]{3,1,0,2:T(8,128)(2,1)S(1)}, u32[]{:S(2)}, u32[]{:S(2)}) collective-permute-start(bf16[32,32,1,128]{3,1,0,2:T(8,128)(2,1)} %copy.489), channel_id=1, source_target_pairs={{0,4},{4,8},{8,12},{12,16},{16,20},{20,24},{24,28},{1,5},{5,9},{9,... | collective-permute-start | bytes 786440 | tf_op jit(solution)/shard_map/ppermute | solution.py:23
  9.7 277.7 %collective-permute-start.1 = (bf16[32,32,1,128]{3,1,0,2:T(8,128)(2,1)}, bf16[32,32,1,128]{3,1,0,2:T(8,128)(2,1)}, u32[]{:S(2)}, u32[]{:S(2)}) collective-permute-start(bf16[32,32,1,128]{3,1,0,2:T(8,128)(2,1)} %copy.490), channel_id=1, source_target_pairs={{4,0},{8,4},{12,8},{16,12},{20,16},{24,20},{28,24},{5,1},{9,5},{13... | collective-permute-start | bytes 786440 | tf_op jit(solution)/shard_map/ppermute | solution.py:25
  210.1 24.0 %collective-permute-start.2 = (bf16[32,64,32]{2,0,1:T(8,128)(2,1)}, bf16[32,64,32]{2,0,1:T(8,128)(2,1)}, u32[]{:S(2)}, u32[]{:S(2)}) collective-permute-start(bf16[32,64,32]{2,0,1:T(8,128)(2,1)} %bitcast.301), channel_id=1, source_target_pairs={{0,1},{1,2},{2,3},{4,5},{5,6},{6,7},{8,9},{9,10},{10,11},{12,13},{... | collective-permute-start | bytes 393224 | tf_op jit(solution)/shard_map/ppermute | solution.py:176
  215.0 28.2 %collective-permute-start.3 = (bf16[32,64,32]{2,0,1:T(8,128)(2,1)}, bf16[32,64,32]{2,0,1:T(8,128)(2,1)}, u32[]{:S(2)}, u32[]{:S(2)}) collective-permute-start(bf16[32,64,32]{2,0,1:T(8,128)(2,1)} %bitcast.300), channel_id=1, source_target_pairs={{1,0},{2,1},{3,2},{5,4},{6,5},{7,6},{9,8},{10,9},{11,10},{13,12},{... | collective-permute-start | bytes 393224 | tf_op jit(solution)/shard_map/ppermute | solution.py:177
  262.2 83.6 %copy-start = (f32[1,2,8,2,4,4,2]{0,2,6,5,4,3,1:T(8,128)S(1)}, f32[1,2,8,2,4,4,2]{0,2,6,5,4,3,1:T(8,128)}, u32[]{:S(2)}) copy-start(f32[1,2,8,2,4,4,2]{0,2,6,5,4,3,1:T(8,128)} %copy.382) | copy-start | bytes 12292
  288.4 95.2 %copy-start.1 = (f32[32,32]{1,0:T(8,128)S(1)}, f32[32,32]{1,0:T(8,128)}, u32[]{:S(2)}) copy-start(f32[32,32]{1,0:T(8,128)} %get-tuple-element.58) | copy-start | bytes 12292
  288.5 95.2 %copy-start.2 = (f32[32,32]{1,0:T(8,128)S(1)}, f32[32,32]{1,0:T(8,128)}, u32[]{:S(2)}) copy-start(f32[32,32]{1,0:T(8,128)} %get-tuple-element.59) | copy-start | bytes 12292
  288.5 95.2 %copy-start.3 = (f32[32,32]{1,0:T(8,128)S(1)}, f32[32,32]{1,0:T(8,128)}, u32[]{:S(2)}) copy-start(f32[32,32]{1,0:T(8,128)} %get-tuple-element.60) | copy-start | bytes 12292
  288.5 95.2 %copy-start.4 = (f32[32,32]{1,0:T(8,128)S(1)}, f32[32,32]{1,0:T(8,128)}, u32[]{:S(2)}) copy-start(f32[32,32]{1,0:T(8,128)} %get-tuple-element.61) | copy-start | bytes 12292
  288.5 95.2 %copy-start.5 = (f32[32,32]{1,0:T(8,128)S(1)}, f32[32,32]{1,0:T(8,128)}, u32[]{:S(2)}) copy-start(f32[32,32]{1,0:T(8,128)} %get-tuple-element.62) | copy-start | bytes 12292
  305.4 78.3 %copy-start.6 = (f32[32,32]{1,0:T(8,128)S(1)}, f32[32,32]{1,0:T(8,128)}, u32[]{:S(2)}) copy-start(f32[32,32]{1,0:T(8,128)} %get-tuple-element.63) | copy-start | bytes 12292
  305.4 78.3 %copy-start.7 = (f32[32,32]{1,0:T(8,128)S(1)}, f32[32,32]{1,0:T(8,128)}, u32[]{:S(2)}) copy-start(f32[32,32]{1,0:T(8,128)} %get-tuple-element.64) | copy-start | bytes 12292
  305.4 78.3 %copy-start.8 = (f32[32,32]{1,0:T(8,128)S(1)}, f32[32,32]{1,0:T(8,128)}, u32[]{:S(2)}) copy-start(f32[32,32]{1,0:T(8,128)} %get-tuple-element.65) | copy-start | bytes 12292
  341.6 42.1 %copy-start.9 = (f32[32,32]{1,0:T(8,128)S(1)}, f32[32,32]{1,0:T(8,128)}, u32[]{:S(2)}) copy-start(f32[32,32]{1,0:T(8,128)} %get-tuple-element.66) | copy-start | bytes 12292
  345.8 92.7 %copy-start.10 = (pred[128]{0:T(512)(128)(4,1)S(1)}, pred[128]{0:T(512)(128)(4,1)}, u32[]{:S(2)}) copy-start(pred[128]{0:T(512)(128)(4,1)} %get-tuple-element.75) | copy-start | bytes 388
  357.8 14.6 %all-to-all-start = ((f32[8,4,672]{2,1,0:T(4,128)}), f32[8,4,672]{2,1,0:T(4,128)S(1)}, u32[]{:S(2)}, u32[]{:S(2)}) async-start(f32[8,4,672]{2,1,0:T(4,128)} %copy.393), calls=%async_computation | async-start | bytes 196608 | tf_op jit(solution)/shard_map/all_to_all | solution.py:251
  373.0 9.3 %all-to-all-start.1 = ((f32[8,4,672]{2,0,1:T(8,128)}), f32[8,4,672]{2,0,1:T(8,128)S(1)}, u32[]{:S(2)}, u32[]{:S(2)}) async-start(f32[8,4,672]{2,0,1:T(8,128)} %copy.394), calls=%async_computation.1 | async-start | bytes 196608 | tf_op jit(solution)/shard_map/all_to_all | solution.py:250
